TPU v7x, 32 devices: a whole 2x2x4 slice. The times are simulated.
32 devices in a mesh: grp: 4 (over z), orb: 4 (over y, core), slab: 2 (over x).
Axes of the slice: x: 2, y: 2, z: 4, core: 2. Of those that a mesh axis runs over, the one named last changes fastest.
Arguments:
- orbitals: float32 [128, 64, 64, 64], P(('grp', 'orb'), 'slab'), may hold values from -6 to 6
- offsets: int32 [128, 2], replicated, may hold values from 0 to 15
- pairs: int32 [128, 2], P(('grp', 'orb')), may hold values from 0 to 127, as said below
- live: int32 [128], P(('grp', 'orb')), may hold values from 0 to 1, as said below
Outputs:
- exchange: float32 [128, 64, 64, 64], P(('grp', 'orb'), 'slab')
Inputs may be any that keep to these rules, and one draw needn't show every extreme that they name: The 8 rows of one device of grp and orb (aligned blocks, in order) name as first orbital one of that device's 8 orbitals; the second orbital lies within 8 positions of the first on the cycle of 128 orbitals. In every block, row 0 pairs the device's lowest orbital with the orbital just below it on the cycle, and row 1 pairs the device's highest orbital with the orbital just above it. In each aligned block of 8 slots the live ones come first, at least two are live, and some block is all live.
All inputs are finite; a program needn't handle non-finite values.
Results may differ from a plain program's by a relative error of at most 0.0003.
Values sent between devices are 32-bit elements; how exact they have to be, the bound alone decides.
A program may use at most 192 MiB of HBM per device.

v0:
```python
import jax
import jax.numpy as jnp
from jax import lax
from jax.sharding import PartitionSpec as P

PASSES = 8


DIAG = 6.25
THETA = 1.075
DELTA = 0.925


def with_halo(shard, sides, width, wrap):
    for axis, dim in sides:
        size, length = (lax.axis_size(axis), shard.shape[dim])
        up = [(i, (i + 1) % size) for i in range(size if wrap else size - 1)]
        down = [(j, i) for i, j in up]
        last = lax.slice_in_dim(shard, length - width, length, axis=dim)
        leading = lax.slice_in_dim(shard, 0, width, axis=dim)
        before = lax.ppermute(last, axis, up)
        after = lax.ppermute(leading, axis, down)
        shard = jnp.concatenate([before, shard, after], axis=dim)
    return shard


def shifted(shard, axis, by):
    size = lax.axis_size(axis)
    return lax.ppermute(shard, axis, [(i, (i + by) % size) for i in range(size)])


def place_many(field, shift_y, shift_z):
    cells = field.shape[2]
    index = jnp.arange(cells, dtype=jnp.int32)
    move_y = (index[None, :, None] == index[None, None, :] - shift_y[:, None, None]).astype(
        jnp.float32
    )
    move_z = (index[None, :, None] == index[None, None, :] - shift_z[:, None, None]).astype(
        jnp.float32
    )
    moved = jnp.einsum("pxuz,puy->pxyz", field, move_y, precision=lax.Precision.HIGHEST)
    return jnp.einsum("pxyv,pvz->pxyz", moved, move_z, precision=lax.Precision.HIGHEST)


def apply_op(padded):
    core = padded[:, 1:-1]
    wider = jnp.pad(core, ((0, 0), (0, 0), (1, 1), (1, 1)))
    near = padded[:, 2:] + padded[:, :-2]
    near = near + wider[:, :, 2:, 1:-1] + wider[:, :, :-2, 1:-1]
    near = near + wider[:, :, 1:-1, 2:] + wider[:, :, 1:-1, :-2]
    return DIAG * core - near


def smooth(density, widen):
    sigma = THETA / DELTA
    resid = density
    value = jnp.zeros_like(density)
    step = resid / (DIAG * THETA)
    coef = 1.0 / sigma
    for turn in range(PASSES):
        value = value + step
        if turn < PASSES - 1:
            resid = resid - apply_op(widen(step))
            coef_new = 1.0 / (2.0 * sigma - coef)
            step = coef_new * coef * step + 2.0 * coef_new / DELTA * (resid / DIAG)
            coef = coef_new
    return value


def slab_faces(field):
    return with_halo(field, (("slab", 1),), 1, False)


def body(orbitals, offsets, pairs, live):
    orb_dev = orbitals.shape[0]
    slots = pairs.shape[0]
    total_orbs = offsets.shape[0]
    field_shape = orbitals.shape[1:]
    extended = with_halo(orbitals, ((("grp", "orb"), 0),), orb_dev, True)
    start = lax.axis_index(("grp", "orb")) * orb_dev - orb_dev
    first_local = jnp.mod(pairs[:, 0] - start, total_orbs)
    second_local = jnp.mod(pairs[:, 1] - start, total_orbs)
    table_ids = jnp.arange(total_orbs, dtype=jnp.int32)
    pick_first = (pairs[:, 0:1] == table_ids[None, :]).astype(jnp.int32)
    pick_second = (pairs[:, 1:2] == table_ids[None, :]).astype(jnp.int32)
    shift = jnp.sum((pick_second - pick_first)[:, :, None] * offsets[None, :, :], axis=1)
    rows = jnp.arange(3 * orb_dev, dtype=jnp.int32)
    select_first = (rows[:, None] == first_local[None, :]).astype(jnp.float32)
    select_second = (rows[:, None] == second_local[None, :]).astype(jnp.float32)
    flat_ext = extended.reshape(3 * orb_dev, -1)
    own = jnp.dot(select_first.T, flat_ext, precision=lax.Precision.HIGHEST).reshape(
        (slots,) + field_shape
    )
    other = jnp.dot(select_second.T, flat_ext, precision=lax.Precision.HIGHEST).reshape(
        (slots,) + field_shape
    )
    partner = place_many(other, shift[:, 0], shift[:, 1])
    density = own * partner
    potential = smooth(density, slab_faces)
    weight = live.astype(jnp.float32)[:, None, None, None]
    to_first = weight * potential * partner
    to_second = weight * place_many(potential * own, -shift[:, 0], -shift[:, 1])
    summed = jnp.dot(select_first, to_first.reshape(slots, -1), precision=lax.Precision.HIGHEST)
    summed = summed + jnp.dot(
        select_second, to_second.reshape(slots, -1), precision=lax.Precision.HIGHEST
    )
    summed = summed.reshape((3 * orb_dev,) + field_shape)
    before = summed[:orb_dev]
    middle = summed[orb_dev : 2 * orb_dev]
    after = summed[2 * orb_dev :]
    from_next = shifted(before, ("grp", "orb"), -1)
    from_prior = shifted(after, ("grp", "orb"), 1)
    return middle + from_next + from_prior


def solution(mesh):
    placed = (
        P(("grp", "orb"), "slab", None, None),
        P(),
        P(("grp", "orb"), None),
        P(("grp", "orb")),
    )
    return jax.shard_map(
        body,
        mesh=mesh,
        in_specs=placed,
        out_specs=P(("grp", "orb"), "slab", None, None),
        check_vma=False,
    )
```

profile of v0, /device:TPU:27, one launch (start us, length us, event | category | flops | bytes accessed | tf_op | source)
XLA Modules:
  0.0 875.6 jit_solution(2674337667326701700)
XLA Ops:
  4.3 178.1 %collective-permute-done = f32[8,32,64,64]{3,2,1,0:T(8,128)} collective-permute-done((f32[8,32,64,64]{3,2,1,0:T(8,128)}, f32[8,32,64,64]{3,2,1,0:T(8,128)}, u32[]{:S(2)}, u32[]{:S(2)}) %collective-permute-start) | collective-permute-done | bytes 4194336 | tf_op jit(solution)/shard_map/ppermute | solution.py:21
  184.0 17.9 %pad_maximum_fusion = f32[24,32,64,64]{3,2,1,0:T(8,128)} fusion(f32[8,32,64,64]{3,2,1,0:T(8,128)} %collective-permute-done.1, f32[8,32,64,64]{3,2,1,0:T(8,128)} %param.4, f32[8,32,64,64]{3,2,1,0:T(8,128)} %collective-permute-done), kind=kLoop, calls=%fused_computation.1 | loop fusion | flops 6291456 | bytes 25165824 | tf_op jit(solution)/shard_map/concatenate | solution.py:23
  201.8 23.3 %reshape.196 = f32[24,131072]{1,0:T(8,128)} reshape(f32[24,32,64,64]{3,2,1,0:T(8,128)} %pad_maximum_fusion) | data formatting | bytes 25165824 | tf_op jit(solution)/shard_map/reshape | solution.py:90
  225.1 26.2 %dot_general.29 = f32[32,64,64,24]{2,1,0,3:T(8,128)} reshape(f32[131072,24]{0,1:T(8,128)} %bitcast.65) | data formatting | bytes 25165824 | tf_op jit(solution)/shard_map/dot_general | solution.py:91
  251.3 28.3 %fusion = f32[8,32,64,64]{3,0,2,1:T(8,128)S(1)} fusion(f32[32,64,64,24]{2,1,0,3:T(8,128)} %dot_general.29, s32[8]{0:T(128)S(1)} %get-tuple-element.44), kind=kOutput, calls=%fused_computation.2 | convolution fusion | flops 301990080 | bytes 16777248 | tf_op jit(solution)/shard_map/dot_general | solution.py:94
  279.6 5.8 fusion.62
  285.5 6.7 fusion.58
  292.2 39.0 %broadcast_multiply_fusion = (f32[8,32,64,64]{3,0,2,1:T(8,128)}, f32[8,32,64,64]{3,0,2,1:T(8,128)}, f32[8,32,64,64]{3,0,2,1:T(8,128)}) fusion(f32[8,32,64,64]{3,2,1,0:T(8,128)} %fusion.58, f32[32,64,64,24]{2,1,0,3:T(8,128)} %dot_general.29, s32[8]{0:T(128)S(1)} %get-tuple-element.45), kind=kOutput, calls=%fused_computation.104 | convolution fusion | flops 304087232 | bytes 29360160 | tf_op jit(solution)/shard_map/dot_general | solution.py:91
  341.6 23.2 %multiply_add_fusion.5 = (f32[8,32,64,64]{3,0,2,1:T(8,128)S(1)}, f32[8,32,64,64]{3,0,2,1:T(8,128)}) fusion(f32[8,32,64,64]{3,0,2,1:T(8,128)} %get-tuple-element.20, f32[8,32,64,64]{3,0,2,1:T(8,128)} %get-tuple-element.19, f32[8,1,64,64]{3,0,2,1:T(8,128)S(1)} %collective-permute-done.3, f32[8,1,64,64]{3,0,2,1:T(8,128)S(1)} %collective-permute-done.2), kind=kLoop, calls=%fused_computation.100 | loop fusion | flops 13631488 | bytes 17039360 | tf_op jit(solution)/shard_map/add | solution.py:65
  369.6 3.8 collective-permute-done.5
  373.4 12.2 %multiply_add_fusion.4 = (f32[8,32,64,64]{3,0,2,1:T(8,128)}, f32[8,32,64,64]{3,0,2,1:T(8,128)}) fusion(f32[8,32,64,64]{3,0,2,1:T(8,128)S(1)} %get-tuple-element.17, f32[8,32,64,64]{3,0,2,1:T(8,128)} %get-tuple-element.18, f32[8,1,64,64]{3,0,2,1:T(8,128)S(1)} %collective-permute-done.5, f32[8,1,64,64]{3,0,2,1:T(8,128)S(1)} %collective-permute-done.4), kind=kLoop, calls=%fused_computation.97 | loop fusion | flops 13631488 | bytes 17039360 | tf_op jit(solution)/shard_map/add | solution.py:65
  395.3 25.9 %multiply_add_fusion.3 = (f32[8,32,64,64]{3,0,2,1:T(8,128)S(1)}, f32[8,32,64,64]{3,0,2,1:T(8,128)}) fusion(f32[8,32,64,64]{3,0,2,1:T(8,128)} %get-tuple-element.15, f32[8,32,64,64]{3,0,2,1:T(8,128)} %get-tuple-element.16, f32[8,1,64,64]{3,0,2,1:T(8,128)S(1)} %collective-permute-done.7, f32[8,1,64,64]{3,0,2,1:T(8,128)S(1)} %collective-permute-done.6), kind=kLoop, calls=%fused_computation.94 | loop fusion | flops 13631488 | bytes 17039360 | tf_op jit(solution)/shard_map/add | solution.py:65
  429.8 12.2 %multiply_add_fusion.2 = (f32[8,32,64,64]{3,0,2,1:T(8,128)}, f32[8,32,64,64]{3,0,2,1:T(8,128)}) fusion(f32[8,32,64,64]{3,0,2,1:T(8,128)S(1)} %get-tuple-element.13, f32[8,32,64,64]{3,0,2,1:T(8,128)} %get-tuple-element.14, f32[8,1,64,64]{3,0,2,1:T(8,128)S(1)} %collective-permute-done.9, f32[8,1,64,64]{3,0,2,1:T(8,128)S(1)} %collective-permute-done.8), kind=kLoop, calls=%fused_computation.91 | loop fusion | flops 13631488 | bytes 17039360 | tf_op jit(solution)/shard_map/add | solution.py:65
  451.7 25.6 %multiply_add_fusion.1 = (f32[8,32,64,64]{3,0,2,1:T(8,128)S(1)}, f32[8,32,64,64]{3,0,2,1:T(8,128)}) fusion(f32[8,32,64,64]{3,0,2,1:T(8,128)} %get-tuple-element.11, f32[8,32,64,64]{3,0,2,1:T(8,128)} %get-tuple-element.12, f32[8,1,64,64]{3,0,2,1:T(8,128)S(1)} %collective-permute-done.11, f32[8,1,64,64]{3,0,2,1:T(8,128)S(1)} %collective-permute-done.10), kind=kLoop, calls=%fused_computation.88 | loop fusion | flops 13631488 | bytes 17039360 | tf_op jit(solution)/shard_map/add | solution.py:65
  486.0 12.2 %multiply_add_fusion = (f32[8,32,64,64]{3,0,2,1:T(8,128)}, f32[8,32,64,64]{3,0,2,1:T(8,128)}) fusion(f32[8,32,64,64]{3,0,2,1:T(8,128)S(1)} %get-tuple-element.9, f32[8,32,64,64]{3,0,2,1:T(8,128)} %get-tuple-element.10, f32[8,1,64,64]{3,0,2,1:T(8,128)S(1)} %collective-permute-done.13, f32[8,1,64,64]{3,0,2,1:T(8,128)S(1)} %collective-permute-done.12), kind=kLoop, calls=%fused_computation.85 | loop fusion | flops 13631488 | bytes 17039360 | tf_op jit(solution)/shard_map/add | solution.py:65
  507.9 45.4 %fusion.89 = (f32[8,32,64,64]{3,0,2,1:T(8,128)}, f32[8,32,64,64]{3,0,2,1:T(8,128)}) fusion(f32[8,32,64,64]{3,0,2,1:T(8,128)} %get-tuple-element.48, f32[8,32,64,64]{3,0,2,1:T(8,128)} %get-tuple-element.8, f32[8,32,64,64]{3,0,2,1:T(8,128)} %get-tuple-element.7, f32[8,1,64,64]{3,0,2,1:T(8,128)S(1)} %collective-permute-done.15, ...), kind=kLoop, calls=%fused_computation.148 | loop fusion | flops 23068672 | bytes 46399488 | tf_op jit(solution)/shard_map/mul | solution.py:102
  553.3 9.1 %fusion.60 = f32[8,64,32,64]{3,1,2,0:T(8,128)S(1)} fusion(f32[8,32,64,64]{3,0,2,1:T(8,128)} %get-tuple-element.5, s32[8,64]{1,0:T(8,128)S(1)} %get-tuple-element.52), kind=kOutput, calls=%fused_computation.77 | convolution fusion | flops 805339136 | bytes 8390656 | tf_op jit(solution)/shard_map/pxuz,puy->pxyz/dot_general | solution.py:41
  562.4 4.3 fusion.56
  566.7 24.7 %copy_multiply_fusion = (f32[8,32,64,64]{3,0,2,1:T(8,128)}, f32[8,32,64,64]{3,0,2,1:T(8,128)}) fusion(f32[8,32,64,64]{3,2,1,0:T(8,128)S(1)} %fusion.56, f32[8]{0:T(128)S(1)} %convert_element_type.31, f32[8,32,64,64]{3,2,1,0:T(8,128)} %fusion.58, f32[8,32,64,64]{3,0,2,1:T(8,128)} %get-tuple-element.6), kind=kLoop, calls=%fused_computation.76 | loop fusion | flops 3145728 | bytes 20971552 | tf_op jit(solution)/shard_map/mul | solution.py:102
  591.4 8.4 copy.21
  599.8 7.8 reshape.197
  607.5 9.6 %fusion.77 = f32[24,131072]{1,0:T(8,128)} fusion(f32[8,131072]{1,0:T(8,128)} %reshape.197, s32[8]{0:T(128)S(1)} %get-tuple-element.45), kind=kOutput, calls=%fused_computation.128 | convolution fusion | flops 301990080 | bytes 16777248 | tf_op jit(solution)/shard_map/dot_general | solution.py:103
  617.2 8.4 copy.24
  625.6 7.7 reshape.198
  633.2 14.3 %convolution_add_fusion = f32[24,131072]{1,0:T(8,128)} fusion(f32[24,131072]{1,0:T(8,128)} %fusion.77, f32[8,131072]{1,0:T(8,128)} %reshape.198, s32[8]{0:T(128)S(1)} %copy-done.4), kind=kOutput, calls=%fused_computation | convolution fusion | flops 305135808 | bytes 29360160 | tf_op jit(solution)/shard_map/dot_general | solution.py:104
  647.5 9.6 %fusion.97 = (f32[8,131072]{1,0:T(8,128)}, f32[8,131072]{1,0:T(8,128)}, f32[8,131072]{1,0:T(8,128)}) fusion(f32[24,131072]{1,0:T(8,128)} %convolution_add_fusion), kind=kLoop, calls=%fused_computation.149 | loop fusion | bytes 25165824 | tf_op jit(solution)/shard_map/slice | solution.py:108
  657.1 8.7 slice.282
  665.9 8.9 %slice.284 = f32[8,32,64,64]{3,2,1,0:T(8,128)} reshape(f32[8,131072]{1,0:T(8,128)} %get-tuple-element.22) | data formatting | bytes 8388608 | tf_op jit(solution)/shard_map/slice | solution.py:110
  674.8 14.6 %collective-permute-start.17 = (f32[8,32,64,64]{3,2,1,0:T(8,128)}, f32[8,32,64,64]{3,2,1,0:T(8,128)}, u32[]{:S(2)}, u32[]{:S(2)}) collective-permute-start(f32[8,32,64,64]{3,2,1,0:T(8,128)} %slice.284), channel_id=1, source_target_pairs={{0,2},{2,4},{4,6},{6,8},{8,10},{10,12},{12,14},{14,16},{16,18},{18... | collective-permute-start | bytes 12582920 | tf_op jit(solution)/shard_map/ppermute | solution.py:29
  689.4 8.7 slice.280
  698.1 163.5 %collective-permute-done.16 = f32[8,32,64,64]{3,2,1,0:T(8,128)} collective-permute-done((f32[8,32,64,64]{3,2,1,0:T(8,128)}, f32[8,32,64,64]{3,2,1,0:T(8,128)}, u32[]{:S(2)}, u32[]{:S(2)}) %collective-permute-start.16) | collective-permute-done | bytes 4194336 | tf_op jit(solution)/shard_map/ppermute | solution.py:29
  861.6 13.7 %add_add_fusion = f32[8,32,64,64]{3,2,1,0:T(8,128)} fusion(f32[8,32,64,64]{3,2,1,0:T(8,128)} %collective-permute-done.17, f32[8,32,64,64]{3,2,1,0:T(8,128)} %slice.280, f32[8,32,64,64]{3,2,1,0:T(8,128)} %collective-permute-done.16), kind=kLoop, calls=%fused_computation.81 | loop fusion | flops 2097152 | bytes 16777216 | tf_op jit(solution)/shard_map/add | solution.py:113
  (60 shorter events, 67.2 us)
Async XLA Ops:
  0.0 182.4 %collective-permute-start = (f32[8,32,64,64]{3,2,1,0:T(8,128)}, f32[8,32,64,64]{3,2,1,0:T(8,128)}, u32[]{:S(2)}, u32[]{:S(2)}) collective-permute-start(f32[8,32,64,64]{3,2,1,0:T(8,128)} %param.4), channel_id=1, source_target_pairs={{0,2},{2,4},{4,6},{6,8},{8,10},{10,12},{12,14},{14,16},{16,18},{18... | collective-permute-start | bytes 12582920 | tf_op jit(solution)/shard_map/ppermute | solution.py:21
  1.8 182.2 %collective-permute-start.1 = (f32[8,32,64,64]{3,2,1,0:T(8,128)}, f32[8,32,64,64]{3,2,1,0:T(8,128)}, u32[]{:S(2)}, u32[]{:S(2)}) collective-permute-start(f32[8,32,64,64]{3,2,1,0:T(8,128)} %param.4), channel_id=1, source_target_pairs={{2,0},{4,2},{6,4},{8,6},{10,8},{12,10},{14,12},{16,14},{18,16},{20... | collective-permute-start | bytes 12582920 | tf_op jit(solution)/shard_map/ppermute | solution.py:22
  4.2 247.1 %copy-start.3 = (s32[8]{0:T(128)}, s32[8]{0:T(128)S(1)}, u32[]{:S(2)}) copy-start(s32[8]{0:T(128)S(1)} %get-tuple-element.44) | copy-start | bytes 100
  332.3 5.5 collective-permute-start.2
  334.5 7.1 collective-permute-start.3
  364.8 20.8 %copy-start = (f32[8,32,64,64]{3,0,2,1:T(8,128)}, f32[8,32,64,64]{3,0,2,1:T(8,128)S(1)}, u32[]{:S(2)}) copy-start(f32[8,32,64,64]{3,0,2,1:T(8,128)S(1)} %get-tuple-element.17) | copy-start | bytes 12582916
  364.8 4.8 collective-permute-start.4
  366.3 7.1 collective-permute-start.5
  386.7 4.8 collective-permute-start.6
  388.2 7.1 collective-permute-start.7
  421.1 20.9 %copy-start.1 = (f32[8,32,64,64]{3,0,2,1:T(8,128)}, f32[8,32,64,64]{3,0,2,1:T(8,128)S(1)}, u32[]{:S(2)}) copy-start(f32[8,32,64,64]{3,0,2,1:T(8,128)S(1)} %get-tuple-element.13) | copy-start | bytes 12582916
  421.2 4.8 collective-permute-start.8
  422.7 7.1 collective-permute-start.9
  429.8 16.1 %copy-start.5 = (s32[8]{0:T(128)S(1)}, s32[8]{0:T(128)}, u32[]{:S(2)}) copy-start(s32[8]{0:T(128)} %param.7) | copy-start | bytes 100
  443.1 4.8 collective-permute-start.10
  444.6 7.1 collective-permute-start.11
  477.3 20.9 %copy-start.2 = (f32[8,32,64,64]{3,0,2,1:T(8,128)}, f32[8,32,64,64]{3,0,2,1:T(8,128)S(1)}, u32[]{:S(2)}) copy-start(f32[8,32,64,64]{3,0,2,1:T(8,128)S(1)} %get-tuple-element.9) | copy-start | bytes 12582916
  477.4 4.8 collective-permute-start.12
  478.9 7.1 collective-permute-start.13
  499.3 4.8 collective-permute-start.14
  500.8 7.1 collective-permute-start.15
  625.6 7.7 copy-start.4
  665.9 195.7 %collective-permute-start.16 = (f32[8,32,64,64]{3,2,1,0:T(8,128)}, f32[8,32,64,64]{3,2,1,0:T(8,128)}, u32[]{:S(2)}, u32[]{:S(2)}) collective-permute-start(f32[8,32,64,64]{3,2,1,0:T(8,128)} %slice.282), channel_id=1, source_target_pairs={{0,30},{2,0},{4,2},{6,4},{8,6},{10,8},{12,10},{14,12},{16,14},{18,... | collective-permute-start | bytes 12582920 | tf_op jit(solution)/shard_map/ppermute | solution.py:29
  674.8 186.9 %collective-permute-start.17 = (f32[8,32,64,64]{3,2,1,0:T(8,128)}, f32[8,32,64,64]{3,2,1,0:T(8,128)}, u32[]{:S(2)}, u32[]{:S(2)}) collective-permute-start(f32[8,32,64,64]{3,2,1,0:T(8,128)} %slice.284), channel_id=1, source_target_pairs={{0,2},{2,4},{4,6},{6,8},{8,10},{10,12},{12,14},{14,16},{16,18},{18... | collective-permute-start | bytes 12582920 | tf_op jit(solution)/shard_map/ppermute | solution.py:29
where the time goes:
time: 882 us; the launch traced here: 876 us
  waiting for transfers between devices  384 us (44%)
  other arithmetic  215 us (24%)
  local copies, waits for them, and re-layouts  123 us (14%)
  matrix products  117 us (13%)
  starting transfers between devices  36.5 us (4%)
    ppermute x8, waiting for transfers between devices, with_halo(): before = lax.ppermute(last, axis, up)  205 us
    ppermute x2, waiting for transfers between devices, shifted(): lax.ppermute(shard, axis, [(i, (i + by) % size) for i in range(size)])  164 us
    add x6, other arithmetic, smooth(): step = coef_new * coef * step + 2.0 * coef_new / DELTA * (resid / DIAG)  111 us
    mul x2, other arithmetic, body(): to_second = weight * place_many(potential * own, -shift[:, 0], -shift[:, 1])  70.1 us
    dot_general x1, matrix products, body(): jnp.dot(select_first.T, flat_ext, precision=lax.Precision.HIGHEST)  39 us
    dot_general x1, matrix products, body(): jnp.dot(select_second.T, flat_ext, precision=lax.Precision.HIGHEST)  28.3 us
    dot_general x1, local copies, waits for them, and re-layouts, body(): jnp.dot(select_first.T, flat_ext, precision=lax.Precision.HIGHEST)  26.2 us
    reshape x1, local copies, waits for them, and re-layouts, body(): flat_ext = extended.reshape(3 * orb_dev, -1)  23.3 us
  transfers between devices with their start and end apart: 18, of which 17 were waited for; matrix products, arithmetic and copies ran while one was open for 2% of the time, Pallas kernels for 0%

commit v1 on v0

v1 whole, which is shorter than its diff:
```python
import functools

import jax
import jax.numpy as jnp
from jax import lax
from jax.experimental import pallas as pl
from jax.experimental.pallas import tpu as pltpu
from jax.sharding import PartitionSpec as P

PASSES = 8
DIAG = 6.25
THETA = 1.075
DELTA = 0.925
EDGE = PASSES - 1
PAD = 16
CYCLE = ("grp", "orb")
F32 = jnp.float32


def coefs():
    sigma = THETA / DELTA
    coef = 1.0 / sigma
    out = []
    for _ in range(PASSES - 1):
        new = 1.0 / (2.0 * sigma - coef)
        out.append((new * coef, 2.0 * new / (DELTA * DIAG)))
        coef = new
    return out


def lanes(shape):
    return lax.broadcasted_iota(jnp.int32, shape, len(shape) - 1)


def pack_kernel(src, dst):
    half = dst.shape[1]
    dst[0] = jnp.concatenate([src[0, :half], src[0, half:]], axis=-1)


def pack(orbitals):
    n, x, y, z = orbitals.shape
    return pl.pallas_call(
        pack_kernel,
        grid=(n,),
        in_specs=[pl.BlockSpec((1, x, y, z), lambda i: (i, 0, 0, 0))],
        out_specs=pl.BlockSpec((1, x // 2, y, 2 * z), lambda i: (i, 0, 0, 0)),
        out_shape=jax.ShapeDtypeStruct((n, x // 2, y, 2 * z), F32),
        name="pack",
    )(orbitals)


def copy_kernel(idx, src_a, src_b, dst_a, dst_b):
    dst_a[...] = src_a[...]
    dst_b[...] = src_b[...]


def gather(packed, lists, m):
    _, h, y, w = packed.shape
    blk = (1, h, y, w)
    out = jax.ShapeDtypeStruct((m, h, y, w), F32)
    return pl.pallas_call(
        copy_kernel,
        grid_spec=pltpu.PrefetchScalarGridSpec(
            num_scalar_prefetch=1,
            grid=(m,),
            in_specs=[
                pl.BlockSpec(blk, lambda i, idx: (idx[0, i], 0, 0, 0)),
                pl.BlockSpec(blk, lambda i, idx: (idx[1, i], 0, 0, 0)),
            ],
            out_specs=[pl.BlockSpec(blk, lambda i, idx: (i, 0, 0, 0))] * 2,
        ),
        out_shape=[out, out],
        name="gather",
    )(lists, packed, packed)


def place(value, room, a, b):
    y, w = value.shape[1:]
    z = w // 2
    room[:, PAD : PAD + y, :] = value
    moved = room[:, pl.ds(PAD - a, y), :]
    moved = pltpu.roll(moved, lax.rem(b + w, w), axis=2)
    pos = lanes(moved.shape) % z - b
    return jnp.where((pos >= 0) & (pos < z), moved, 0.0)


def clear_room(room):
    y = room.shape[1] - 2 * PAD
    room[:, :PAD, :] = jnp.zeros((room.shape[0], PAD, room.shape[2]), F32)
    room[:, PAD + y :, :] = jnp.zeros((room.shape[0], PAD, room.shape[2]), F32)


def density_kernel(plan, own, mine, prior, nxt, partner, density, low, high, room):
    p = pl.program_id(0)
    kind = plan[4, p]
    a, b = plan[5, p], plan[6, p]

    @pl.when(p == 0)
    def _():
        clear_room(room)

    def go(src):
        part = place(src[0], room, a, b)
        partner[0] = part
        dens = own[0] * part
        density[0] = dens
        h, y, w = dens.shape
        flat = jnp.concatenate([dens[..., : w // 2], dens[..., w // 2 :]], axis=0)
        top, bot = flat[:EDGE], flat[2 * h - EDGE :]
        low[0] = jnp.concatenate([top[:, : y // 2], top[:, y // 2 :]], axis=-1)
        high[0] = jnp.concatenate([bot[:, : y // 2], bot[:, y // 2 :]], axis=-1)

    for value, src in enumerate((mine, prior, nxt)):
        pl.when(kind == value)(functools.partial(go, src))


def densities(plan, packed, prior, nxt):
    slots = plan.shape[1]
    _, h, y, w = packed.shape
    blk = (1, h, y, w)
    eblk = (1, EDGE, y // 2, w)

    def at(row):
        return pl.BlockSpec(blk, lambda i, plan: (plan[row, i], 0, 0, 0))

    full = jax.ShapeDtypeStruct((slots, h, y, w), F32)
    edge = jax.ShapeDtypeStruct((slots,) + eblk[1:], F32)
    here = lambda i, plan: (i, 0, 0, 0)
    return pl.pallas_call(
        density_kernel,
        grid_spec=pltpu.PrefetchScalarGridSpec(
            num_scalar_prefetch=1,
            grid=(slots,),
            in_specs=[at(0), at(1), at(2), at(3)],
            out_specs=[
                pl.BlockSpec(blk, here),
                pl.BlockSpec(blk, here),
                pl.BlockSpec(eblk, here),
                pl.BlockSpec(eblk, here),
            ],
            scratch_shapes=[pltpu.VMEM((h, y + 2 * PAD, w), F32)],
        ),
        out_shape=[full, full, edge, edge],
        name="density",
    )(plan, packed, packed, prior, nxt)


def solve_kernel(
    plan, ends, density, partner, own, below, above,
    acc, acc_prior, acc_next, resid, step_a, step_b, total, mask, room,
):
    p = pl.program_id(0)
    h, y, w = density.shape[1:]
    z = w // 2
    rows = h + 2 * EDGE

    @pl.when(p == 0)
    def _():
        clear_room(room)
        for ref in (acc, acc_prior, acc_next):
            ref[...] = jnp.zeros(ref.shape, F32)
        for ref in (step_a, step_b):
            ref[:, :8, :] = jnp.zeros((rows, 8, w), F32)
            ref[:, 8 + y :, :] = jnp.zeros((rows, 8, w), F32)
        lane = lanes((1, w))
        first = ends[0] == 0
        last = ends[0] == ends[1] - 1
        for t in range(rows):
            plane = jnp.where(lane < z, t - EDGE, t - EDGE + h)
            outside = ((plane < 0) & first) | ((plane >= 2 * h) & last)
            mask[t] = jnp.where(outside, 0.0, 1.0)

    @pl.when(plan[7, p] > 0)
    def _():
        def unfold(part):
            return jnp.concatenate([part[..., :z], part[..., z:]], axis=1)

        dens = density[0]
        line = jnp.concatenate(
            [unfold(below[0]), dens[..., :z], dens[..., z:], unfold(above[0])], axis=0
        )
        resid[...] = jnp.concatenate([line[:rows], line[h:]], axis=-1)
        step_a[:, 8 : 8 + y, :] = resid[...] * (1.0 / (DIAG * THETA))
        total[...] = step_a[EDGE : EDGE + h, 8 : 8 + y, :]
        lane = lanes((y, w)) % z
        not_low = lane > 0
        not_high = lane < z - 1
        bufs = [step_a, step_b]
        for turn, (keep, gain) in enumerate(coefs()):
            now, then = bufs[turn % 2], bufs[1 - turn % 2]
            core_only = turn == PASSES - 2

            def row(t, now=now, then=then, keep=keep, gain=gain, last=core_only):
                core = now[t, 8 : 8 + y, :]
                near = now[t - 1, 8 : 8 + y, :] + now[t + 1, 8 : 8 + y, :]
                near = near + now[t, 7 : 7 + y, :] + now[t, 9 : 9 + y, :]
                near = near + jnp.where(not_low, pltpu.roll(core, 1, axis=1), 0.0)
                near = near + jnp.where(not_high, pltpu.roll(core, w - 1, axis=1), 0.0)
                left = resid[t] - (DIAG * core - near)
                fresh = (keep * core + gain * left) * mask[t]
                if not last:
                    resid[t] = left
                    then[t, 8 : 8 + y, :] = fresh
                return fresh

            lo, hi = turn + 1, rows - turn - 1

            def outer(t, c):
                row(t)
                return c

            def inner(t, c):
                total[t - EDGE] += row(t)
                return c

            if lo < EDGE:
                lax.fori_loop(lo, EDGE, outer, 0)
                lax.fori_loop(EDGE + h, hi, outer, 0)
            lax.fori_loop(EDGE, EDGE + h, inner, 0)

        pot = total[...]
        acc[plan[0, p]] += pot * partner[0]
        back = place(pot * own[0], room, -plan[5, p], -plan[6, p])
        for value, ref in enumerate((acc, acc_prior, acc_next)):

            @pl.when(plan[4, p] == value)
            def _(ref=ref, value=value):
                ref[plan[1 + value, p]] += back


def solve(plan, ends, density, partner, packed, below, above, m):
    slots = plan.shape[1]
    n, h, y, w = packed.shape
    blk = (1, h, y, w)
    eblk = (1, EDGE, y // 2, w)
    rows = h + 2 * EDGE
    here = lambda i, plan, ends: (i, 0, 0, 0)
    fixed = lambda i, plan, ends: (0, 0, 0, 0)
    shapes = [(n, h, y, w), (m, h, y, w), (m, h, y, w)]
    return pl.pallas_call(
        solve_kernel,
        grid_spec=pltpu.PrefetchScalarGridSpec(
            num_scalar_prefetch=2,
            grid=(slots,),
            in_specs=[
                pl.BlockSpec(blk, here),
                pl.BlockSpec(blk, here),
                pl.BlockSpec(blk, lambda i, plan, ends: (plan[0, i], 0, 0, 0)),
                pl.BlockSpec(eblk, here),
                pl.BlockSpec(eblk, here),
            ],
            out_specs=[pl.BlockSpec(s, fixed) for s in shapes],
            scratch_shapes=[
                pltpu.VMEM((rows, y, w), F32),
                pltpu.VMEM((rows, y + 16, w), F32),
                pltpu.VMEM((rows, y + 16, w), F32),
                pltpu.VMEM((h, y, w), F32),
                pltpu.VMEM((rows, 1, w), F32),
                pltpu.VMEM((h, y + 2 * PAD, w), F32),
            ],
        ),
        out_shape=[jax.ShapeDtypeStruct(s, F32) for s in shapes],
        compiler_params=pltpu.CompilerParams(vmem_limit_bytes=56 * 1024 * 1024),
        name="solve",
    )(plan, ends, density, partner, packed, below, above)


def combine_kernel(back, acc, from_next, from_prior, out):
    k = pl.program_id(0)
    h = acc.shape[1]
    z = acc.shape[3] // 2
    value = acc[0]
    value = value + jnp.where(back[1, k] > 0, from_next[0], 0.0)
    value = value + jnp.where(back[3, k] > 0, from_prior[0], 0.0)
    out[0, :h] = value[:, :, :z]
    out[0, h:] = value[:, :, z:]


def combine(back, acc, from_next, from_prior):
    n, h, y, w = acc.shape
    blk = (1, h, y, w)
    return pl.pallas_call(
        combine_kernel,
        grid_spec=pltpu.PrefetchScalarGridSpec(
            num_scalar_prefetch=1,
            grid=(n,),
            in_specs=[
                pl.BlockSpec(blk, lambda i, back: (i, 0, 0, 0)),
                pl.BlockSpec(blk, lambda i, back: (back[0, i], 0, 0, 0)),
                pl.BlockSpec(blk, lambda i, back: (back[2, i], 0, 0, 0)),
            ],
            out_specs=pl.BlockSpec((1, 2 * h, y, w // 2), lambda i, back: (i, 0, 0, 0)),
        ),
        out_shape=jax.ShapeDtypeStruct((n, 2 * h, y, w // 2), F32),
        name="combine",
    )(back, acc, from_next, from_prior)


def cycle(field, by):
    size = lax.axis_size(CYCLE)
    return lax.ppermute(field, CYCLE, [(i, (i + by) % size) for i in range(size)])


def body(orbitals, offsets, pairs, live):
    n = orbitals.shape[0]
    slots = pairs.shape[0]
    total = offsets.shape[0]
    blocks = total // n
    slabs = lax.axis_size("slab")
    me = lax.axis_index(CYCLE)
    packed = pack(orbitals)

    mine = jnp.concatenate([pairs, live[:, None]], axis=1)
    every = lax.all_gather(mine, CYCLE, axis=0)
    ids = jnp.arange(blocks, dtype=jnp.int32)
    second = every[:, :, 1]
    alive = every[:, :, 2] > 0
    orb = jnp.arange(n, dtype=jnp.int32)
    sides = jnp.stack([(ids - 1) % blocks, (ids + 1) % blocks])
    hit = alive[None] & (second[None] // n == sides[:, :, None])
    need = jnp.any(
        hit[..., None] & (second[None, :, :, None] % n == orb), axis=2
    )
    count = jnp.sum(need.astype(jnp.int32), axis=2)
    most = jnp.max(count)

    after, before = (me + 1) % blocks, (me - 1) % blocks
    flags = jnp.stack(
        [need[0, me], need[1, me], need[0, after], need[1, before]]
    ).astype(jnp.int32)
    spot = jnp.sum(
        flags[:, None, :] * (orb[None, :] < orb[:, None]).astype(jnp.int32)[None], axis=2
    )
    lists = jnp.sum(
        (flags[:, None, :] * (spot[:, None, :] == orb[None, :, None])) * orb, axis=2
    )
    back = jnp.stack(
        [spot[2] * flags[2], flags[2], spot[3] * flags[3], flags[3]]
    )

    i, j, on = pairs[:, 0], pairs[:, 1], live > 0
    owner, local = j // n, j % n
    pick_j = (local[:, None] == orb[None, :]).astype(jnp.int32)
    from_prior = (owner == before) & on
    from_next = (owner == after) & on
    kind = jnp.where(from_prior, 1, jnp.where(from_next, 2, 0))
    where_prior = jnp.sum(pick_j * spot[0][None, :], axis=1) * from_prior
    where_next = jnp.sum(pick_j * spot[1][None, :], axis=1) * from_next
    ids_all = jnp.arange(total, dtype=jnp.int32)
    diff = (j[:, None] == ids_all).astype(jnp.int32) - (i[:, None] == ids_all).astype(jnp.int32)
    shift = jnp.sum(diff[:, :, None] * offsets[None], axis=1)
    plan = jnp.stack(
        [i % n, local, where_prior, where_next, kind, shift[:, 0], shift[:, 1], live]
    ).astype(jnp.int32)
    ends = jnp.stack([lax.axis_index("slab"), slabs]).astype(jnp.int32)

    up = [(s, s + 1) for s in range(slabs - 1)]
    down = [(s + 1, s) for s in range(slabs - 1)]

    def branch(m):
        def run(_):
            to_next, to_prior = gather(packed, lists[2:], m)
            prior = cycle(to_next, 1)
            nxt = cycle(to_prior, -1)
            partner, density, low, high = densities(plan, packed, prior, nxt)
            below = lax.ppermute(high, "slab", up)
            above = lax.ppermute(low, "slab", down)
            acc, acc_prior, acc_next = solve(
                plan, ends, density, partner, packed, below, above, m
            )
            return combine(back, acc, cycle(acc_prior, -1), cycle(acc_next, 1))

        return run

    sizes = sorted({min(s, slots - 1) for s in (2, 3, 4, 5)} | {slots - 1})
    which = sum((most > s).astype(jnp.int32) for s in sizes[:-1])
    return lax.switch(which, [branch(s) for s in sizes], 0)


def solution(mesh):
    placed = (
        P(CYCLE, "slab", None, None),
        P(),
        P(CYCLE, None),
        P(CYCLE),
    )
    return jax.shard_map(
        body,
        mesh=mesh,
        in_specs=placed,
        out_specs=P(CYCLE, "slab", None, None),
        check_vma=False,
    )
```

time: 882 us -> 264 us (0.30)
  the two profiles are of different devices: /device:TPU:27 before, /device:TPU:16 now
where the time goes in v1:
time: 264 us; the launch traced here: 268 us
  waiting for transfers between devices  112 us (42%)
  Pallas kernels  88.2 us (33%)
  starting transfers between devices  37.7 us (14%)
  blocking collectives  16.1 us (6%)
  other arithmetic  5.82 us (2%)
  local copies, waits for them, and re-layouts  5.39 us (2%)
  between operations  2.7 us (1%)
    ppermute x4, waiting for transfers between devices, cycle(): lax.ppermute(field, CYCLE, [(i, (i + by) % size) for i in range(size)])  97.7 us
    pallas_call x1, Pallas kernels, solve(): pl.pallas_call(solve_kernel, grid_spec=pltpu.PrefetchScalarGridSpec(num_s...  55.3 us
    ppermute x4, starting transfers between devices, cycle(): lax.ppermute(field, CYCLE, [(i, (i + by) % size) for i in range(size)])  33 us
    all_gather x1, blocking collectives, body(): every = lax.all_gather(mine, CYCLE, axis=0)  16.1 us
    pallas_call x1, Pallas kernels, densities(): pl.pallas_call(density_kernel, grid_spec=pltpu.PrefetchScalarGridSpec(num...  10.9 us
    ppermute x1, waiting for transfers between devices, run(): below = lax.ppermute(high, 'slab', up)  9.85 us
    pallas_call x1, Pallas kernels, combine(): pl.pallas_call(combine_kernel, grid_spec=pltpu.PrefetchScalarGridSpec(num...  9.3 us
    pallas_call x1, Pallas kernels, pack(): pl.pallas_call(pack_kernel, grid=(n,), in_specs=[pl.BlockSpec((1, x, y, z...  8.13 us
  transfers between devices with their start and end apart: 6, of which 5 were waited for; matrix products, arithmetic and copies ran while one was open for 0% of the time, Pallas kernels for 0%

profile of v1, /device:TPU:16, one launch (start us, length us, event | category | flops | bytes accessed | tf_op | source)
XLA Modules:
  0.0 267.8 jit_solution(13013804962493616726)
XLA Ops:
  0.1 0.8 and_select_fusion.2
  0.8 0.7 select_bitcast_fusion
  1.6 0.8 slice_bitcast_fusion.5
  2.3 0.7 add_bitcast_fusion
  3.1 0.8 multiply_reduce_fusion.1
  4.0 16.1 %all-gather.1 = s32[16,8,3]{1,2,0:T(4,128)S(1)} all-gather(s32[1,8,3]{1,2,0:T(4,128)S(1)} %add_bitcast_fusion), channel_id=2, replica_groups=mesh['grp'=4,'orb'=4,'slab'=2] {'grp','orb'}, dimensions={0}, use_global_device_ids=true | all-gather | bytes 1632 | tf_op jit(solution)/shard_map/all_gather | solution.py:314
  20.3 0.2 dynamic-slice_reduce_fusion.3
  20.6 0.6 reduce_max.9
  24.0 0.2 select_reduce_fusion
  24.2 0.7 select_bitcast_fusion.1
  24.9 0.7 stack.54
  25.5 8.1 %pack.1 = f32[8,16,64,128]{3,2,1,0:T(8,128)} custom-call(f32[8,32,64,64]{3,2,1,0:T(8,128)} %src.1), custom_call_target="tpu_custom_call" | custom-call | tf_op jit(solution)/shard_map/pack/pallas_call | solution.py:42
  33.7 234.2 %conditional.1 = (f32[8,32,64,64]{3,2,1,0:T(8,128)}) conditional(s32[]{:T(128)} %clamp.3, (s32[4,8]{1,0:T(4,128)S(1)}, f32[8,16,64,128]{3,2,1,0:T(8,128)}, s32[8,8]{1,0:T(8,128)S(1)}, s32[2]{0:T(128)S(1)}, s32[4,8]{1,0:T(4,128)S(1)}, /*index=5*/s32[]{:T(128)}, s32[4,8,8]{2,1,0:T(8,128)S(1)}, ...), branch_computations={%region_8.9_spmd, %region_9.10_spmd, %region_10.11_spmd, %region_1... | conditional | flops 992 | bytes 77598448 | solution.py:377
  33.7 0.1 fusion.1
  33.8 0.6 slice.38.idx
  34.4 4.6 %gather.6 = (f32[3,16,64,128]{3,2,1,0:T(8,128)}, f32[3,16,64,128]{3,2,1,0:T(8,128)}) custom-call(s32[2,8]{1,0:T(2,128)} %slice.38.idx, f32[8,16,64,128]{3,2,1,0:T(8,128)} %get-tuple-element.78.src_a.src_b.own.mine, f32[8,16,64,128]{3,2,1,0:T(8,128)} %get-tuple-element.78.src_a.src_b.own.mine), custom_call_target="tpu_custom_call" | custom-call | tf_op jit(solution)/shard_map/cond/branch_1_fun/gather/pallas_call | solution.py:61
  39.0 2.6 collective-permute-start.7
  41.6 18.4 %collective-permute-done.6.prior = f32[3,16,64,128]{3,2,1,0:T(8,128)S(1)} collective-permute-done((f32[3,16,64,128]{3,2,1,0:T(8,128)}, f32[3,16,64,128]{3,2,1,0:T(8,128)S(1)}, u32[]{:S(2)}, u32[]{:S(2)}) %collective-permute-start.6) | collective-permute-done | bytes 1572896 | tf_op jit(solution)/shard_map/cond/branch_1_fun/ppermute | solution.py:301
  60.0 1.2 copy-done.6
  61.2 0.5 copy-done.7
  61.7 10.9 %density.6 = (f32[8,16,64,128]{3,2,1,0:T(8,128)}, f32[8,16,64,128]{3,2,1,0:T(8,128)}, f32[8,7,32,128]{3,2,1,0:T(8,128)}, f32[8,7,32,128]{3,2,1,0:T(8,128)}) custom-call(s32[8,8]{1,0:T(8,128)S(1)} %get-tuple-element.76.plan, f32[8,16,64,128]{3,2,1,0:T(8,128)} %get-tuple-element.78.src_a.src_b.own.mine, ...), custom_call_target="tpu_custom_call" | custom-call | tf_op jit(solution)/shard_map/cond/branch_1_fun/density/pallas_call | solution.py:129
  72.6 3.4 %collective-permute-start.8 = (f32[8,7,32,128]{3,2,1,0:T(8,128)}, f32[8,7,32,128]{3,2,1,0:T(8,128)S(1)}, u32[]{:S(2)}, u32[]{:S(2)}) collective-permute-start(f32[8,7,32,128]{3,2,1,0:T(8,128)} %get-tuple-element.84), channel_id=1, source_target_pairs={{0,1},{2,3},{4,5},{6,7},{8,9},{10,11},{12,13},{14,15},{16,17},{18,... | collective-permute-start | bytes 2752520 | tf_op jit(solution)/shard_map/cond/branch_1_fun/ppermute | solution.py:366
  76.0 1.3 collective-permute-start.9
  77.3 9.9 %collective-permute-done.8.below = f32[8,7,32,128]{3,2,1,0:T(8,128)S(1)} collective-permute-done((f32[8,7,32,128]{3,2,1,0:T(8,128)}, f32[8,7,32,128]{3,2,1,0:T(8,128)S(1)}, u32[]{:S(2)}, u32[]{:S(2)}) %collective-permute-start.8) | collective-permute-done | bytes 917536 | tf_op jit(solution)/shard_map/cond/branch_1_fun/ppermute | solution.py:366
  87.2 4.3 %collective-permute-done.9.above = f32[8,7,32,128]{3,2,1,0:T(8,128)S(1)} collective-permute-done((f32[8,7,32,128]{3,2,1,0:T(8,128)}, f32[8,7,32,128]{3,2,1,0:T(8,128)S(1)}, u32[]{:S(2)}, u32[]{:S(2)}) %collective-permute-start.9) | collective-permute-done | bytes 917536 | tf_op jit(solution)/shard_map/cond/branch_1_fun/ppermute | solution.py:367
  91.5 0.9 copy-done.18
  92.5 55.3 %solve.6 = (f32[8,16,64,128]{3,2,1,0:T(8,128)}, f32[3,16,64,128]{3,2,1,0:T(8,128)}, f32[3,16,64,128]{3,2,1,0:T(8,128)}) custom-call(s32[8,8]{1,0:T(8,128)S(1)} %get-tuple-element.76.plan, s32[2]{0:T(128)S(1)} %get-tuple-element.77.ends, f32[8,16,64,128]{3,2,1,0:T(8,128)} %get-tuple-element.82.density, f32[8,16,64,128]{3,2,1,0:T(8,128)} %get-tuple-element.83.partner, ...), custom_call_target="tpu_custom_call" | custom-call | tf_op jit(solution)/shard_map/cond/branch_1_fun/solve/pallas_call | solution.py:240
  147.8 30.3 %collective-permute-start.10 = (f32[3,16,64,128]{3,2,1,0:T(8,128)}, f32[3,16,64,128]{3,2,1,0:T(8,128)S(1)}, u32[]{:S(2)}, u32[]{:S(2)}) collective-permute-start(f32[3,16,64,128]{3,2,1,0:T(8,128)} %get-tuple-element.87), channel_id=1, source_target_pairs={{0,30},{2,0},{4,2},{6,4},{8,6},{10,8},{12,10},{14,12},{16,14},{18,... | collective-permute-start | bytes 4718600 | tf_op jit(solution)/shard_map/cond/branch_1_fun/ppermute | solution.py:301
  178.1 18.2 %collective-permute-done.10.from_next = f32[3,16,64,128]{3,2,1,0:T(8,128)S(1)} collective-permute-done((f32[3,16,64,128]{3,2,1,0:T(8,128)}, f32[3,16,64,128]{3,2,1,0:T(8,128)S(1)}, u32[]{:S(2)}, u32[]{:S(2)}) %collective-permute-start.10) | collective-permute-done | bytes 1572896 | tf_op jit(solution)/shard_map/cond/branch_1_fun/ppermute | solution.py:301
  196.3 61.0 %collective-permute-done.11.from_prior = f32[3,16,64,128]{3,2,1,0:T(8,128)S(1)} collective-permute-done((f32[3,16,64,128]{3,2,1,0:T(8,128)}, f32[3,16,64,128]{3,2,1,0:T(8,128)S(1)}, u32[]{:S(2)}, u32[]{:S(2)}) %collective-permute-start.11) | collective-permute-done | bytes 1572896 | tf_op jit(solution)/shard_map/cond/branch_1_fun/ppermute | solution.py:301
  257.4 1.1 copy-done.5
  258.5 9.3 %combine.6 = f32[8,32,64,64]{3,2,1,0:T(8,128)} custom-call(s32[4,8]{1,0:T(4,128)S(1)} %get-tuple-element.75.back, f32[8,16,64,128]{3,2,1,0:T(8,128)} %get-tuple-element.86.acc, f32[3,16,64,128]{3,2,1,0:T(8,128)} %copy-done.4, f32[3,16,64,128]{3,2,1,0:T(8,128)} %copy-done.5), custom_call_target="tpu_custom_call" | custom-call | tf_op jit(solution)/shard_map/cond/branch_1_fun/combine/pallas_call | solution.py:282
  (33 shorter events, 0.6 us)
Async XLA Ops:
  39.0 21.1 %collective-permute-start.6 = (f32[3,16,64,128]{3,2,1,0:T(8,128)}, f32[3,16,64,128]{3,2,1,0:T(8,128)S(1)}, u32[]{:S(2)}, u32[]{:S(2)}) collective-permute-start(f32[3,16,64,128]{3,2,1,0:T(8,128)} %get-tuple-element.80), channel_id=1, source_target_pairs={{0,2},{2,4},{4,6},{6,8},{8,10},{10,12},{12,14},{14,16},{16,18},{18... | collective-permute-start | bytes 4718600 | tf_op jit(solution)/shard_map/cond/branch_1_fun/ppermute | solution.py:301
  39.0 21.1 %collective-permute-start.7 = (f32[3,16,64,128]{3,2,1,0:T(8,128)}, f32[3,16,64,128]{3,2,1,0:T(8,128)S(1)}, u32[]{:S(2)}, u32[]{:S(2)}) collective-permute-start(f32[3,16,64,128]{3,2,1,0:T(8,128)} %get-tuple-element.81), channel_id=1, source_target_pairs={{0,30},{2,0},{4,2},{6,4},{8,6},{10,8},{12,10},{14,12},{16,14},{18,... | collective-permute-start | bytes 4718600 | tf_op jit(solution)/shard_map/cond/branch_1_fun/ppermute | solution.py:301
  60.0 1.2 copy-start.6
  60.0 1.7 copy-start.7
  72.6 14.6 %collective-permute-start.8 = (f32[8,7,32,128]{3,2,1,0:T(8,128)}, f32[8,7,32,128]{3,2,1,0:T(8,128)S(1)}, u32[]{:S(2)}, u32[]{:S(2)}) collective-permute-start(f32[8,7,32,128]{3,2,1,0:T(8,128)} %get-tuple-element.84), channel_id=1, source_target_pairs={{0,1},{2,3},{4,5},{6,7},{8,9},{10,11},{12,13},{14,15},{16,17},{18,... | collective-permute-start | bytes 2752520 | tf_op jit(solution)/shard_map/cond/branch_1_fun/ppermute | solution.py:366
  76.0 15.5 %collective-permute-start.9 = (f32[8,7,32,128]{3,2,1,0:T(8,128)}, f32[8,7,32,128]{3,2,1,0:T(8,128)S(1)}, u32[]{:S(2)}, u32[]{:S(2)}) collective-permute-start(f32[8,7,32,128]{3,2,1,0:T(8,128)} %get-tuple-element.85), channel_id=1, source_target_pairs={{1,0},{3,2},{5,4},{7,6},{9,8},{11,10},{13,12},{15,14},{17,16},{19,... | collective-permute-start | bytes 2752520 | tf_op jit(solution)/shard_map/cond/branch_1_fun/ppermute | solution.py:367
  87.2 4.3 %copy-start.13 = (f32[8,7,32,128]{3,2,1,0:T(8,128)}, f32[8,7,32,128]{3,2,1,0:T(8,128)S(1)}, u32[]{:S(2)}) copy-start(f32[8,7,32,128]{3,2,1,0:T(8,128)S(1)} %collective-permute-done.8.below) | copy-start | bytes 2752516 | tf_op jit(solution)/shard_map/cond
  91.5 0.9 copy-start.18
  147.8 48.6 %collective-permute-start.10 = (f32[3,16,64,128]{3,2,1,0:T(8,128)}, f32[3,16,64,128]{3,2,1,0:T(8,128)S(1)}, u32[]{:S(2)}, u32[]{:S(2)}) collective-permute-start(f32[3,16,64,128]{3,2,1,0:T(8,128)} %get-tuple-element.87), channel_id=1, source_target_pairs={{0,30},{2,0},{4,2},{6,4},{8,6},{10,8},{12,10},{14,12},{16,14},{18,... | collective-permute-start | bytes 4718600 | tf_op jit(solution)/shard_map/cond/branch_1_fun/ppermute | solution.py:301
  178.1 79.3 %collective-permute-start.11 = (f32[3,16,64,128]{3,2,1,0:T(8,128)}, f32[3,16,64,128]{3,2,1,0:T(8,128)S(1)}, u32[]{:S(2)}, u32[]{:S(2)}) collective-permute-start(f32[3,16,64,128]{3,2,1,0:T(8,128)} %get-tuple-element.88), channel_id=1, source_target_pairs={{0,2},{2,4},{4,6},{6,8},{8,10},{10,12},{12,14},{14,16},{16,18},{18... | collective-permute-start | bytes 4718600 | tf_op jit(solution)/shard_map/cond/branch_1_fun/ppermute | solution.py:301
  196.3 61.1 %copy-start.4 = (f32[3,16,64,128]{3,2,1,0:T(8,128)}, f32[3,16,64,128]{3,2,1,0:T(8,128)S(1)}, u32[]{:S(2)}) copy-start(f32[3,16,64,128]{3,2,1,0:T(8,128)S(1)} %collective-permute-done.10.from_next) | copy-start | bytes 4718596 | tf_op jit(solution)/shard_map/cond
  257.4 1.1 copy-start.5
